TPU v7x, 32 devices: a whole 2x2x4 slice. The times are simulated.
32 devices in a mesh: row: 4 (over y, core), col: 4 (over z), feat: 2 (over x).
Axes of the slice: x: 2, y: 2, z: 4, core: 2. Of those that a mesh axis runs over, the one named last changes fastest.
Arguments:
- src_feats: bfloat16 [8192, 256], P(('row', 'col'), 'feat'), may hold values from -170 to 170
- dst_feats: bfloat16 [1024, 256], P(('row', 'col'), 'feat'), may hold values from -170 to 170
- proj: bfloat16 [256, 256], P('feat'), may hold values from -0.375 to 0.375
- att_src: float32 [256], P('feat'), may hold values from -1 to 1
- att_dst: float32 [256], P('feat'), may hold values from -1 to 1
- bias: float32 [256], P('feat'), may hold values from -3 to 3
- tile_rows: int32 [4, 4, 128], P('row', 'col'), may hold values from 0 to 1, as said below
- tile_cols: int32 [4, 4, 128], P('row', 'col'), may hold values from 0 to 15
- tile_count: int32 [4, 4], P('row', 'col'), may hold values from 16 to 128, as said below
- edge_weight: bfloat16 [4, 4, 128, 128, 128], P('row', 'col'), may hold values from 0 to 3, as said below
Outputs:
- node_out: bfloat16 [1024, 256], P(('row', 'col'), 'feat')
Inputs may be any that keep to these rules, and one draw needn't show every extreme that they name: `tile_count`: one device holds exactly 128 live slots in every draw; counts differ several times between devices. `tile_rows`: the slots of one device name distinct tiles as long as there are tiles left in its block, then name the same tiles again in the same order; slots beyond the count also hold valid tile numbers. `edge_weight`: about a third of the entries are edges.
All inputs are finite; a program needn't handle non-finite values.
Results may differ from a plain program's by a relative error of at most 0.001.
Values sent between devices are 32-bit elements; how exact they have to be, the bound alone decides.
No kernel may reach another device: no remote copies, remote signals or barrier semaphores. Data moves between devices by JAX's collectives and lax.ppermute only.
A program may use at most 64 MiB of HBM per device.

v0:
```python
import jax
import jax.numpy as jnp
from jax import lax
from jax.experimental import pallas as pl
from jax.experimental.pallas import tpu as pltpu
from jax.sharding import PartitionSpec as P

HEADS = 8
TILE = 128
SLOPE = 0.2
LOG2E = 1.4426950408889634
NEG = -1e30
F32 = jnp.float32
BF16 = jnp.bfloat16
HIGHEST = lax.Precision.HIGHEST
VMEM = pl.BlockSpec(memory_space=pltpu.VMEM)
SMEM = pl.BlockSpec(memory_space=pltpu.SMEM)
HBM = pl.BlockSpec(memory_space=pltpu.HBM)


def is_pow2(n):
    return n & (n - 1) == 0


def goes_to(i, d, n):
    return i ^ d if is_pow2(n) else lax.rem(i + d, n)


def comes_from(i, d, n):
    return i ^ d if is_pow2(n) else lax.rem(i + n - d, n)


def hop(x, axis, d):
    n = lax.axis_size(axis)
    pairs = [(i, i ^ d if is_pow2(n) else (i + d) % n) for i in range(n)]
    return lax.ppermute(x, axis, pairs)


def call(kernel, out_shape, *args, in_specs=None, flops=0, bytes_accessed=0, grant=8 << 20, **kw):
    return pl.pallas_call(
        kernel,
        out_shape=out_shape,
        in_specs=in_specs or [VMEM] * len(args),
        cost_estimate=pl.CostEstimate(
            flops=flops, bytes_accessed=bytes_accessed, transcendentals=0
        ),
        compiler_params=pltpu.CompilerParams(vmem_limit_bytes=grant),
        **kw,
    )(*args)


def limit(mib, least):
    return min(max(mib << 20, least), 60 << 20)


def in_hbm(x):
    return pltpu.with_memory_space_constraint(x, pltpu.HBM)


def up8(n):
    return -(-n // 8) * 8


def head_rows(vector, heads, width, height):
    dims = width // heads
    shape = (height, width)
    row = lax.broadcasted_iota(jnp.int32, shape, 0) % heads
    lane = lax.broadcasted_iota(jnp.int32, shape, 1)
    return jnp.where(lane // dims == row, jnp.broadcast_to(vector, shape), 0.0)


def contract(lhs, rhs, dims, precision=HIGHEST):
    return lax.dot_general(
        lhs, rhs, (dims, ((), ())), preferred_element_type=F32, precision=precision
    )


def take_cols(proj_ref, which, width):
    if width % TILE == 0:
        return proj_ref[:, pl.ds(pl.multiple_of(which * width, width), width)]
    full = proj_ref[...]
    out = full[:, :width]
    for k in range(1, full.shape[1] // width):
        out = jnp.where(which == k, full[:, k * width : (k + 1) * width], out)
    return out


def project(x, w):
    return lax.dot_general(x, w, (((1,), (0,)), ((), ())), preferred_element_type=F32)


def leaky(x):
    return jnp.maximum(x, SLOPE * x)


def on_device(
    src_feats, dst_feats, proj, att_src, att_dst, bias, tile_rows, tile_cols, tile_count, edge_weight
):
    n_row, n_col, n_feat = (lax.axis_size(a) for a in ("row", "col", "feat"))
    width = proj.shape[1] // n_feat
    heads = HEADS // n_feat
    dims = width // heads
    lanes = -(-width // TILE) * TILE
    src_rows, own_rows = src_feats.shape[0], dst_feats.shape[0]
    slots = tile_rows.shape[2]
    row_tiles = own_rows * n_col // TILE
    piece_tiles = src_rows // TILE
    n_chunk = 2 if piece_tiles % 2 == 0 else 1
    chunk_tiles = piece_tiles // n_chunk
    part_rows = src_rows // n_chunk
    col_tiles = piece_tiles * n_row
    hp = up8(2 * heads)
    mdp = up8(2 * heads)
    att_src2, att_dst2, bias2 = (v.reshape(1, width) for v in (att_src, att_dst, bias))

    def fetch(hbm, vmem, sems):
        copies = [pltpu.make_async_copy(h, v, sems.at[k]) for k, (h, v) in enumerate(zip(hbm, vmem))]
        for copy in copies:
            copy.start()
        for copy in copies:
            copy.wait()

    def fetching(kernel, outs, *args):
        return call(
            kernel,
            outs,
            *map(in_hbm, args),
            in_specs=[HBM] * len(args),
            scratch_shapes=[
                *(pltpu.VMEM(v.shape, v.dtype) for v in args),
                pltpu.SemaphoreType.DMA((len(args),)),
            ],
        )

    def send_kernel(*refs):
        hbm, outs, refs = refs[:4], refs[4:-5], refs[-5:]
        fetch(hbm, refs[:4], refs[4])
        src_ref, dst_ref, proj_ref, att_ref = refs[:4]
        me = lax.axis_index("feat")
        outs[0][...] = project(dst_ref[...], take_cols(proj_ref, me, width))
        outs[1][...] = LOG2E * head_rows(att_ref[...], heads, width, up8(heads))
        for d in range(1, n_feat):
            w = take_cols(proj_ref, goes_to(me, d, n_feat), width)
            own_outs = outs[2 + (d - 1) * (n_chunk + 1) : 2 + d * (n_chunk + 1)]
            own_outs[0][...] = project(dst_ref[...], w)
            for ch in range(n_chunk):
                own_outs[ch + 1][...] = project(src_ref[ch * part_rows : (ch + 1) * part_rows], w)

    dst_own, dst_att, *sent = fetching(
        send_kernel,
        [pltpu.VMEM((own_rows, width), F32), pltpu.VMEM((up8(heads), width), F32)]
        + [
            pltpu.VMEM((n, width), F32)
            for _ in range(1, n_feat)
            for n in [own_rows] + [part_rows] * n_chunk
        ],
        src_feats,
        dst_feats,
        proj,
        att_dst2,
    )
    sent = [sent[k :: n_chunk + 1] for k in range(n_chunk + 1)]
    dst_parts = [hop(sent[0][d - 1], "feat", d) for d in range(1, n_feat)]
    src_parts = [[hop(part[d - 1], "feat", d) for d in range(1, n_feat)] for part in sent[1:]]

    tiles = row_tiles * col_tiles
    whole = lambda shape: pl.BlockSpec(shape, lambda s: (0,) * len(shape))

    def dst_kernel(own_ref, att_ref, *rest):
        got, (z_ref, s_ref) = rest[: n_feat - 1], rest[n_feat - 1 :]
        z = own_ref[...]
        for part in got:
            z = z + part[...]
        z_ref[...] = z
        s_ref[...] = contract(att_ref[...], z, ((1,), (1,)))

    zdst, s_dst = call(
        dst_kernel,
        [
            jax.ShapeDtypeStruct((own_rows, width), F32),
            jax.ShapeDtypeStruct((up8(heads), own_rows), F32),
        ],
        dst_own,
        dst_att,
        *dst_parts,
    )
    rows_of = up8(heads)
    if is_pow2(n_col) and n_col > 1:
        bits = n_col.bit_length() - 1
        place = lambda d: sum(((d >> k) & 1) << (bits - 1 - k) for k in range(bits))
        targets, d = [s_dst], n_col // 2
        while d:
            targets = [targets[0], hop(targets[0], "col", d)]
            d //= 2
            if d:

                def join_kernel(low_ref, high_ref, out_ref):
                    out_ref[...] = jnp.concatenate([low_ref[...], high_ref[...]], axis=0)

                shape = (2 * targets[0].shape[0], own_rows)
                targets = [call(join_kernel, pltpu.VMEM(shape, F32), *targets)]
    else:
        place = lambda d: d
        targets = [s_dst] + [hop(s_dst, "col", d) for d in range(1, n_col)]
    size = n_col // len(targets)

    units = n_row * n_chunk
    period = min(slots, tiles) if slots % min(slots, tiles) == 0 else slots
    reps = slots // period
    group = 8
    groups = period // group
    panel_bytes = 4 * tiles * TILE * TILE
    n_panel = 2 if groups % 2 == 0 and panel_bytes <= 4 << 20 else 1
    share = groups // n_panel

    def weight_sums(first, extra, hbm, small_refs, count_ref, panel_ref, w_ref, sems, w_sems):
        rows_ref, cols_ref = small_refs[-2:]
        small = [
            pltpu.make_async_copy(h, v, sems.at[k]) for k, (h, v) in enumerate(zip(hbm, small_refs))
        ]
        large = [
            pltpu.make_async_copy(
                hbm[-1].at[k, pl.ds((first + g) * group, group)],
                w_ref.at[k, pl.ds(g * group, group)],
                w_sems.at[g, k],
            )
            for g in range(share)
            for k in range(reps)
        ]
        for copy in small + large:
            copy.start()

        @pl.loop(0, units)
        def _(u):
            @pl.loop(0, row_tiles)
            def _(r):
                panel_ref[u, r] = jnp.zeros((chunk_tiles, TILE, TILE), F32)

        for copy in small:
            copy.wait()
        extra()
        row = lax.axis_index("row")
        count = count_ref[0, 0]
        for g in range(share):
            for copy in large[g * reps : (g + 1) * reps]:
                copy.wait()
            base = (first + g) * group

            @pl.loop(base, jnp.clip(count, base, base + group))
            def _(u):
                at = u - first * group
                r, c = rows_ref[0, 0, u], cols_ref[0, 0, u]
                unit = ((c // piece_tiles) ^ row) * n_chunk + c % piece_tiles // chunk_tiles
                t = c % chunk_tiles
                total = w_ref[0, at].astype(F32)
                for k in range(1, reps):
                    live = (u + k * period < count).astype(F32)
                    total = total + w_ref[k, at].astype(F32) * live
                panel_ref[unit, r, t] = panel_ref[unit, r, t] + total

    def local_kernel(*refs):
        hbm, count_ref, refs = refs[:6], refs[6], refs[7:]
        outs, panel_ref, refs = refs[: 1 + n_chunk], refs[1 + n_chunk], refs[2 + n_chunk :]
        src_ref, proj_ref, att_ref = refs[:3]

        def own():
            outs[0][...] = LOG2E * head_rows(att_ref[...], heads, width, hp)
            w = take_cols(proj_ref, lax.axis_index("feat"), width)
            for ch in range(n_chunk):
                outs[1 + ch][...] = project(src_ref[ch * part_rows : (ch + 1) * part_rows], w)

        weight_sums(0, own, hbm, refs[:5], count_ref, panel_ref, *refs[5:])

    def more_kernel(*refs):
        hbm, count_ref, panel_ref, refs = refs[:3], refs[3], refs[4], refs[5:]
        weight_sums(share, lambda: None, hbm, refs[:2], count_ref, panel_ref, *refs[2:])

    def weights(kernel, outs, *inputs):
        return call(
            kernel,
            outs + [pltpu.VMEM((units, row_tiles, chunk_tiles, TILE, TILE), F32)],
            *map(in_hbm, inputs),
            tile_count,
            in_specs=[HBM] * len(inputs) + [SMEM],
            scratch_shapes=[
                *(
                    (pltpu.SMEM if v.dtype == jnp.int32 else pltpu.VMEM)(v.shape, v.dtype)
                    for v in inputs[:-1]
                ),
                pltpu.VMEM((reps, share * group, TILE, TILE), edge_weight.dtype),
                pltpu.SemaphoreType.DMA((len(inputs) - 1,)),
                pltpu.SemaphoreType.DMA((share, reps)),
            ],
            grant=12 << 20,
        )

    slot_weights = edge_weight.reshape(reps, period, TILE, TILE)
    slot_inputs = (tile_rows, tile_cols, slot_weights)
    src_att, *src_own, panel = weights(
        local_kernel,
        [pltpu.VMEM((hp, width), F32)] + [pltpu.VMEM((part_rows, width), F32)] * n_chunk,
        src_feats,
        proj,
        att_src2,
        *slot_inputs,
    )
    panels = [panel]
    if n_panel > 1:
        panels += weights(more_kernel, [], *slot_inputs)

    pack_rows = part_rows + chunk_tiles * hp

    def z_kernel(own_ref, att_ref, *rest):
        got, out_ref = rest[: n_feat - 1], rest[n_feat - 1]
        z = own_ref[...]
        for part in got:
            z = z + part[...]
        if width < lanes:
            out_ref[...] = jnp.zeros_like(out_ref)
        out_ref[:part_rows, :width] = z
        s = contract(att_ref[...], z, ((1,), (1,)))
        low = lax.broadcasted_iota(jnp.int32, s.shape, 0) < heads
        s = jnp.where(low, s, SLOPE * s)
        for t in range(chunk_tiles):
            at = part_rows + t * hp
            out_ref[at : at + hp, :TILE] = s[:, t * TILE : (t + 1) * TILE]

    parts, far_first = {}, n_row // 2
    for ch in range(n_chunk):
        shape = pltpu.VMEM((pack_rows, lanes), F32)
        own = call(z_kernel, shape, src_own[ch], src_att, *src_parts[ch])
        parts[far_first, ch] = hop(own, "row", far_first)
        parts[0, ch] = own

    def spread(first, ch):
        d = n_row // 4
        while d:
            for k in [k for k, c in parts if c == ch and k ^ first < far_first]:
                parts[k ^ d, ch] = hop(parts[k, ch], "row", d)
            d //= 2

    for ch in range(n_chunk):
        spread(0, ch)

    block = 64
    blocks = TILE // block
    unroll = 2 if row_tiles % 2 == 0 else 1
    steps = row_tiles // unroll
    chunk_rows = own_rows + mdp
    group_rows = unroll * TILE
    all_rows = row_tiles * TILE
    tiny, huge = 2.0**-60, 2.0**60
    lane_w = lambda: lax.broadcasted_iota(jnp.int32, (block, width), 1) // dims
    lane_t = lambda: lax.broadcasted_iota(jnp.int32, (block, TILE), 1)

    def score_rows(part_ref, t, h):
        at = part_rows + t * hp + h
        return part_ref[at : at + 1, :TILE], part_ref[at + heads : at + heads + 1, :TILE]

    def panel_sum(refs, rt, t, rows):
        total = refs[0][0, rt, t, rows, :]
        for ref in refs[1:]:
            total = total + ref[0, rt, t, rows, :]
        return total

    def by_unit(refs):
        return [refs[k : k + n_panel] for k in range(0, len(refs), n_panel)]

    def split(x):
        hi = x.astype(BF16)
        return hi, (x - hi.astype(F32)).astype(BF16)

    def split_z(part_refs):
        return jnp.concatenate(
            [jnp.concatenate(split(p[:part_rows, :width]), axis=1) for p in part_refs], axis=0
        )

    def stack(pairs):
        return jnp.concatenate(
            [jnp.concatenate([p[k] for p in row], axis=1) for row in pairs for k in range(2)], axis=0
        )

    def weighted(probs, z):
        both = lax.dot_general(probs, z, (((1,), (0,)), ((), ())), preferred_element_type=F32)
        num = jnp.zeros((block, width), F32)
        for h in range(heads):
            hi = both[2 * h * block : (2 * h + 1) * block]
            lo = both[(2 * h + 1) * block : (2 * h + 2) * block]
            num = jnp.where(lane_w() == h, hi[:, :width] + (hi[:, width:] + lo[:, :width]), num)
        return num

    def attend(part_refs, w_refs, posneg, den_in, num_in, den_out, num_out):
        base = pl.program_id(0) * group_rows
        z_cat = split_z(part_refs)
        for b in range(unroll * blocks):
            at = pl.ds(pl.multiple_of(base + b * block, block), block)
            rt, i0 = divmod(b * block, TILE)
            pairs = []
            for h in range(heads):
                pairs.append([])
                pn = posneg[at, :]
                pos = jnp.broadcast_to(pn[:, h : h + 1], (block, TILE))
                neg = jnp.broadcast_to(pn[:, heads + h : heads + h + 1], (block, TILE))
                den = jnp.zeros((block, TILE), F32) if den_in is None else den_in[h, at, :]
                for k, part_ref in enumerate(part_refs):
                    for t in range(chunk_tiles):
                        s, s_low = score_rows(part_ref, t, h)
                        x = jnp.maximum(pos + s, neg + s_low)
                        p = panel_sum(w_refs[k], rt, t, slice(i0, i0 + block)) * jnp.exp2(x)
                        den = den + p
                        pairs[h].append(split(p))
                den_out[h, at, :] = den
            num = weighted(stack(pairs), z_cat)
            num_out[at, :] = num if num_in is None else num_in[at, :] + num

    shape_t, shape_w, shape_d = (all_rows, TILE), (all_rows, width), (heads, all_rows, TILE)
    part_spec = whole((pack_rows, lanes))

    def unit_spec(k, ch):
        return pl.BlockSpec(
            (1, unroll, chunk_tiles, TILE, TILE), lambda s: (k * n_chunk + ch, s, 0, 0, 0)
        )

    def stage(kernel, keys, before, before_shapes, outs, extra=(), scratch=()):
        n = len(keys)
        return pl.pallas_call(
            kernel,
            out_shape=[pltpu.VMEM(s, F32) for s in outs],
            grid=(steps,),
            in_specs=[whole(s) for s in before_shapes]
            + [part_spec] * (n + len(extra))
            + [unit_spec(*key) for key in (*keys, *extra) for _ in panels],
            out_specs=[whole(s) for s in outs],
            scratch_shapes=scratch,
            cost_estimate=pl.CostEstimate(
                flops=all_rows * n * part_rows * width * heads * 8,
                bytes_accessed=n * part_rows * width * 4,
                transcendentals=all_rows * n * part_rows * heads,
            ),
            compiler_params=pltpu.CompilerParams(vmem_limit_bytes=limit(16, 4 * tiles * TILE * TILE)),
        )(*before, *(parts[key] for key in (*keys, *extra)), *panels * (n + len(extra)))

    near_keys = [(k, ch) for ch in range(n_chunk) for k in range(far_first)]

    def near_kernel(*refs):
        n = len(near_keys)
        n_tgt = len(targets)
        tgt_refs, part_refs, refs = refs[:n_tgt], refs[n_tgt : n_tgt + n], refs[n_tgt + n :]
        w_refs, refs = by_unit(refs[: n * n_panel]), refs[n * n_panel :]
        posneg, tgt_m, den_out, num_out = refs
        col = lax.axis_index("col")

        @pl.when(pl.program_id(0) == 0)
        def _():
            shape = (up8(heads), TILE)
            eye = (
                lax.broadcasted_iota(jnp.int32, shape, 0)
                == lax.broadcasted_iota(jnp.int32, shape, 1) % heads
            ).astype(F32)
            lane = lax.broadcasted_iota(jnp.int32, (1, TILE), 1)
            bound = jnp.zeros((1, TILE), F32)
            for h in range(heads):
                rows = [score_rows(r, t, h)[0] for r in part_refs for t in range(chunk_tiles)]
                top = rows[0]
                for other in rows[1:]:
                    top = jnp.maximum(top, other)
                top = jnp.max(top, axis=1, keepdims=True)
                bound = jnp.where(lane % heads == h, top, bound)
            for d in range(n_col):
                at = pl.ds(
                    pl.multiple_of(comes_from(col, d, n_col) * own_rows, own_rows), own_rows
                )
                k, g = divmod(place(d), size)
                a = contract(tgt_refs[k][g * rows_of : (g + 1) * rows_of], eye, ((0,), (0,)))
                m = leaky(a + bound)
                tgt_m[at, :] = jnp.where(lane < heads, a, m)
                posneg[at, :] = jnp.where(lane < heads, a, SLOPE * a) - m

        attend(part_refs, w_refs, posneg, None, None, den_out, num_out)

    def middle_kernel(*refs):
        n = len(middle_keys)
        (posneg, den_in, num_in), refs = refs[:3], refs[3:]
        part_refs, refs = refs[:n], refs[n:]
        w_refs, (den_out, num_out) = by_unit(refs[: n * n_panel]), refs[n * n_panel :]
        attend(part_refs, w_refs, posneg, den_in, num_in, den_out, num_out)

    def last_kernel(*refs):
        n, n_all = len(last_keys), len(last_keys) + len(other_keys)
        (posneg, den_in, num_in, tgt_m), refs = refs[:4], refs[4:]
        part_refs, refs = refs[:n_all], refs[n_all:]
        w_refs, refs = by_unit(refs[: n_all * n_panel]), refs[n_all * n_panel :]
        out_refs, (den_s, num_s, md_s) = refs[:n_col], refs[n_col:]
        col = lax.axis_index("col")
        step = pl.program_id(0)

        attend(part_refs[:n], w_refs[:n], posneg, den_in, num_in, den_s, num_s)
        base = step * group_rows
        low = high = None
        for b in range(unroll * blocks):
            at = pl.ds(pl.multiple_of(base + b * block, block), block)
            md = tgt_m[at, :]
            for h in range(heads):
                den = jnp.sum(den_s[h, at, :], axis=1, keepdims=True)
                low = den if low is None else jnp.minimum(low, den)
                high = den if high is None else jnp.maximum(high, den)
                md = jnp.where(lane_t() == h, den, md)
            md_s[at, :] = md
        fine = jnp.logical_and(jnp.min(low) >= tiny, jnp.max(high) <= huge)

        @pl.when(jnp.logical_not(fine))
        def _():
            @pl.loop(0, unroll * blocks)
            def _(b):
                at = pl.ds(pl.multiple_of(base + b * block, block), block)
                rt = b // blocks
                rows = pl.ds(pl.multiple_of((b % blocks) * block, block), block)
                md = tgt_m[at, :]
                posnegs, dens = [], []
                for h in range(heads):
                    best = jnp.full((block, TILE), NEG, F32)
                    for part_ref, w_ref in zip(part_refs, w_refs):
                        for t in range(chunk_tiles):
                            edge = panel_sum(w_ref, rt, t, rows) > 0
                            s = score_rows(part_ref, t, h)[0]
                            best = jnp.maximum(best, jnp.where(edge, s, NEG))
                    a = tgt_m[at, :][:, h : h + 1]
                    m = leaky(a + jnp.max(best, axis=1, keepdims=True))
                    md = jnp.where(lane_t() == heads + h, m, md)
                    posnegs.append((a - m, SLOPE * a - m))
                    dens.append(jnp.zeros((block, TILE), F32))
                num_s[at, :] = jnp.zeros((block, width), F32)
                for part_ref, w_ref in zip(part_refs, w_refs):
                    pairs = []
                    for h in range(heads):
                        pairs.append([])
                        pos, neg = posnegs[h]
                        for t in range(chunk_tiles):
                            s, s_low = score_rows(part_ref, t, h)
                            x = jnp.minimum(jnp.maximum(pos + s, neg + s_low), 0.0)
                            p = panel_sum(w_ref, rt, t, rows) * jnp.exp2(x)
                            dens[h] = dens[h] + p
                            pairs[h].append(split(p))
                    num_s[at, :] = num_s[at, :] + weighted(stack(pairs), split_z([part_ref]))
                for h in range(heads):
                    md = jnp.where(lane_t() == h, jnp.sum(dens[h], axis=1, keepdims=True), md)
                md_s[at, :] = md

        @pl.when(step == steps - 1)
        def _():
            for d in range(n_col):
                at = pl.ds(
                    pl.multiple_of(goes_to(col, d, n_col) * own_rows, own_rows), own_rows
                )
                if width < lanes:
                    out_refs[d][...] = jnp.zeros_like(out_refs[d])
                out_refs[d][:own_rows, :width] = num_s[at, :]
                out_refs[d][own_rows:, :own_rows] = md_s[at, :].T[:mdp]

    posneg, tgt_m, den, num = stage(
        near_kernel,
        near_keys,
        targets,
        [(size * rows_of, own_rows)] * len(targets),
        [shape_t, shape_t, shape_d, shape_w],
    )
    arrived = [parts[far_first, ch] for ch in range(n_chunk)]
    arrived, den = lax.optimization_barrier((arrived, den))
    for ch in range(n_chunk):
        parts[far_first, ch] = arrived[ch]
        spread(far_first, ch)
    far_keys = [(k, ch) for k in range(far_first, n_row) for ch in range(n_chunk)]
    middle_keys = far_keys[:n_chunk] if n_row > 2 else []
    if middle_keys:
        den, num = stage(
            middle_kernel,
            middle_keys,
            (posneg, den, num),
            [shape_t, shape_d, shape_w],
            [shape_d, shape_w],
        )
    last_keys = far_keys[len(middle_keys) :]
    other_keys = near_keys + middle_keys
    chunks = stage(
        last_kernel,
        last_keys,
        (posneg, den, num, tgt_m),
        [shape_t, shape_d, shape_w, shape_t],
        [(chunk_rows, lanes)] * n_col,
        extra=other_keys,
        scratch=[
            pltpu.VMEM(shape_d, F32),
            pltpu.VMEM(shape_w, F32),
            pltpu.VMEM(shape_t, F32),
        ],
    )
    gathered = [hop(chunks[d], "col", d) for d in range(n_col - 1, 0, -1)]
    gathered = [chunks[0]] + gathered[::-1]

    def out_kernel(zdst_ref, src_ref, dst_ref, bias_ref, *rest):
        parts, out_ref = rest[:n_col], rest[n_col]
        same = (
            lax.broadcasted_iota(jnp.int32, (width, width), 0) // dims
            == lax.broadcasted_iota(jnp.int32, (width, width), 1) // dims
        ).astype(F32)
        z = zdst_ref[...]
        pair = contract(z * (dst_ref[...] + src_ref[...]), same, ((1,), (0,)))
        e_self = leaky(LOG2E * pair)
        which = lax.broadcasted_iota(jnp.int32, (mdp, width), 0)
        head = lax.broadcasted_iota(jnp.int32, (mdp, width), 1) // dims
        den_of, m_of = (which == head).astype(F32), (which == head + heads).astype(F32)
        mds = [part[own_rows:, :own_rows] for part in parts]
        ms = [contract(md, m_of, ((0,), (0,))) for md in mds]
        dens = [contract(md, den_of, ((0,), (0,))) for md in mds]
        top = e_self
        for m in ms:
            top = jnp.maximum(top, m)
        den = jnp.exp2(e_self - top)
        num = den * z
        for part, m, own_den in zip(parts, ms, dens):
            factor = jnp.exp2(m - top)
            den = den + factor * own_den
            num = num + factor * part[:own_rows, :width]
        x = num / den + bias_ref[...]
        out_ref[...] = jnp.where(x > 0, x, jnp.exp(jnp.minimum(x, 0.0)) - 1.0).astype(BF16)

    return call(
        out_kernel,
        jax.ShapeDtypeStruct((own_rows, width), BF16),
        zdst,
        att_src2,
        att_dst2,
        bias2,
        *gathered,
    )


def solution(mesh):
    return jax.shard_map(
        on_device,
        mesh=mesh,
        in_specs=(
            P(("row", "col"), "feat"),
            P(("row", "col"), "feat"),
            P("feat", None),
            P("feat"),
            P("feat"),
            P("feat"),
            P("row", "col", None),
            P("row", "col", None),
            P("row", "col"),
            P("row", "col", None, None, None),
        ),
        out_specs=P(("row", "col"), "feat"),
        check_vma=False,
    )
```

profile of v0, /device:TPU:0, one launch (start us, length us, event | category | flops | bytes accessed | tf_op | source)
XLA Modules:
  0.0 45.5 jit_solution(705616383031828420)
XLA Ops:
  0.0 1.2 %shard_map.100 = (f32[64,128]{1,0:T(8,128)S(1)}, f32[8,128]{1,0:T(8,128)S(1)}, f32[64,128]{1,0:T(8,128)S(1)}, f32[256,128]{1,0:T(8,128)S(1)}, f32[256,128]{1,0:T(8,128)S(1)}) custom-call(bf16[512,128]{1,0:T(8,128)(2,1)} %refs_0_.4, bf16[64,128]{1,0:T(8,128)(2,1)} %refs_1_.3, bf16[128,256]{1,0:T(8,128)(2,1)} %refs_1_.4, f32[1,128]{1,0:T(1,128)} %bitcast.4), custom_call_target="tpu_custom_call" | custom-call | tf_op jit(solution)/shard_map/pallas_call | solution.py:40
  1.2 3.0 %collective-permute-start.5 = (f32[256,128]{1,0:T(8,128)S(1)}, f32[256,128]{1,0:T(8,128)S(1)}, u32[]{:S(2)}, u32[]{:S(2)}) collective-permute-start(f32[256,128]{1,0:T(8,128)S(1)} %get-tuple-element.38), channel_id=1, source_target_pairs={{0,1},{1,0},{2,3},{3,2},{4,5},{5,4},{6,7},{7,6},{8,9},{9,8},{10,11... | collective-permute-start | bytes 393224 | tf_op jit(solution)/shard_map/ppermute | solution.py:36
  4.2 0.1 collective-permute-start.3
  4.9 2.0 %shard_map.103 = (f32[8,128]{1,0:T(8,128)S(1)}, f32[256,128]{1,0:T(8,128)S(1)}, f32[256,128]{1,0:T(8,128)S(1)}, f32[8,2,2,128,128]{4,3,2,1,0:T(8,128)S(1)}) custom-call(bf16[512,128]{1,0:T(8,128)(2,1)} %refs_0_.4, bf16[128,256]{1,0:T(8,128)(2,1)} %refs_1_.4, f32[1,128]{1,0:T(1,128)} %bitcast.6, s32[1,1,128]{2,1,0:T(1,128)} %refs_0_.5, s32[1,1,128]{2,1,0:T(1,128)} %refs_1_.5, ...), custom_call_target="tpu_custom_call" | custom-call | tf_op jit(solution)/shard_map/pallas_call | solution.py:40
  6.9 1.6 %collective-permute-done.5.rest_0_ = f32[256,128]{1,0:T(8,128)S(1)} collective-permute-done((f32[256,128]{1,0:T(8,128)S(1)}, f32[256,128]{1,0:T(8,128)S(1)}, u32[]{:S(2)}, u32[]{:S(2)}) %collective-permute-start.5) | collective-permute-done | bytes 131104 | tf_op jit(solution)/shard_map/ppermute | solution.py:36
  8.6 0.2 shard_map.105.refs_4_.refs_8_
  8.8 0.0 collective-permute-start.6
  8.8 1.8 %collective-permute-done.3.rest_0_ = f32[256,128]{1,0:T(8,128)S(1)} collective-permute-done((f32[256,128]{1,0:T(8,128)S(1)}, f32[256,128]{1,0:T(8,128)S(1)}, u32[]{:S(2)}, u32[]{:S(2)}) %collective-permute-start.3) | collective-permute-done | bytes 131104 | tf_op jit(solution)/shard_map/ppermute | solution.py:36
  10.5 0.2 shard_map.104.refs_2_.refs_6_
  10.7 1.8 %collective-permute-start = (f32[64,128]{1,0:T(8,128)S(1)}, f32[64,128]{1,0:T(8,128)S(1)}, u32[]{:S(2)}, u32[]{:S(2)}) collective-permute-start(f32[64,128]{1,0:T(8,128)S(1)} %get-tuple-element.31), channel_id=1, source_target_pairs={{0,1},{1,0},{2,3},{3,2},{4,5},{5,4},{6,7},{7,6},{8,9},{9,8},{10,11... | collective-permute-start | bytes 98312 | tf_op jit(solution)/shard_map/ppermute | solution.py:36
  12.5 1.5 %collective-permute-start.8 = (f32[272,128]{1,0:T(8,128)S(1)}, f32[272,128]{1,0:T(8,128)S(1)}, u32[]{:S(2)}, u32[]{:S(2)}) collective-permute-start(f32[272,128]{1,0:T(8,128)S(1)} %shard_map.105.refs_4_.refs_8_), channel_id=1, source_target_pairs={{0,16},{8,24},{16,0},{24,8},{1,17},{9,25},{17,1},{25,9},{2,18},{10... | collective-permute-start | bytes 417800 | tf_op jit(solution)/shard_map/ppermute | solution.py:36
  14.0 0.5 %collective-permute-start.7 = (f32[272,128]{1,0:T(8,128)S(1)}, f32[272,128]{1,0:T(8,128)S(1)}, u32[]{:S(2)}, u32[]{:S(2)}) collective-permute-start(f32[272,128]{1,0:T(8,128)S(1)} %shard_map.104.refs_2_.refs_6_), channel_id=1, source_target_pairs={{0,16},{8,24},{16,0},{24,8},{1,17},{9,25},{17,1},{25,9},{2,18},{10... | collective-permute-start | bytes 417800 | tf_op jit(solution)/shard_map/ppermute | solution.py:36
  14.5 0.1 collective-permute-done.rest_0_
  14.7 0.1 shard_map.101
  14.8 2.9 %collective-permute-start.1 = (f32[8,64]{1,0:T(8,128)S(1)}, f32[8,64]{1,0:T(8,128)S(1)}, u32[]{:S(2)}, u32[]{:S(2)}) collective-permute-start(f32[8,64]{1,0:T(8,128)S(1)} %get-tuple-element.33.low_ref), channel_id=1, source_target_pairs={{0,4},{2,6},{4,0},{6,2},{1,5},{3,7},{5,1},{7,3},{8,12},{10,14},{12... | collective-permute-start | bytes 6152 | tf_op jit(solution)/shard_map/ppermute | solution.py:36
  17.7 1.7 %collective-permute-done.1.high_ref = f32[8,64]{1,0:T(8,128)S(1)} collective-permute-done((f32[8,64]{1,0:T(8,128)S(1)}, f32[8,64]{1,0:T(8,128)S(1)}, u32[]{:S(2)}, u32[]{:S(2)}) %collective-permute-start.1) | collective-permute-done | bytes 2080 | tf_op jit(solution)/shard_map/ppermute | solution.py:36
  19.4 1.8 %collective-permute-start.2 = (f32[16,64]{1,0:T(8,128)S(1)}, f32[16,64]{1,0:T(8,128)S(1)}, u32[]{:S(2)}, u32[]{:S(2)}) collective-permute-start(f32[16,64]{1,0:T(8,128)S(1)} %shard_map.102.refs_0_), channel_id=1, source_target_pairs={{0,2},{2,0},{4,6},{6,4},{1,3},{3,1},{5,7},{7,5},{8,10},{10,8},{12,... | collective-permute-start | bytes 12296 | tf_op jit(solution)/shard_map/ppermute | solution.py:36
  21.2 1.8 %shard_map.106.refs_7_.refs_9_.refs_11_.refs_13_.refs_6_.refs_8_.refs_15_.refs_17_.refs_19_.refs_21_.refs_23_.refs_25_.refs_27_ = f32[8,2,2,128,128]{4,3,2,1,0:T(8,128)S(1)} custom-call(s32[1,1,128]{2,1,0:T(1,128)} %refs_0_.5, s32[1,1,128]{2,1,0:T(1,128)} %refs_1_.5, bf16[4,32,128,128]{3,2,1,0:T(8,128)(2,1)} %bitcast.10, s32[1,1]{1,0:T(1,128)S(6)} %copy.11.refs_6_.refs_3_), custom_call_target="tpu_custom_call" | custom-call | tf_op jit(solution)/shard_map/pallas_call | solution.py:40
  23.0 0.0 collective-permute-done.2.refs_1_
  23.0 2.1 %shard_map.107 = (f32[256,128]{1,0:T(8,128)S(1)}, f32[256,128]{1,0:T(8,128)S(1)}, f32[4,256,128]{2,1,0:T(8,128)S(1)}, f32[256,128]{1,0:T(8,128)S(1)}) custom-call(f32[16,64]{1,0:T(8,128)S(1)} %shard_map.102.refs_0_, f32[16,64]{1,0:T(8,128)S(1)} %collective-permute-done.2.refs_1_, f32[272,128]{1,0:T(8,128)S(1)} %shard_map.104.refs_2_.refs_6_, ...), custom_call_target="tpu_custom_call" | custom-call | flops 1073741824 | bytes 524288 | tf_op jit(solution)/shard_map/pallas_call | solution.py:426
  25.1 0.1 collective-permute-start.9
  25.2 0.5 %collective-permute-start.10 = (f32[272,128]{1,0:T(8,128)S(1)}, f32[272,128]{1,0:T(8,128)S(1)}, u32[]{:S(2)}, u32[]{:S(2)}) collective-permute-start(f32[272,128]{1,0:T(8,128)S(1)} %collective-permute-done.8.refs_4_.refs_11_), channel_id=1, source_target_pairs={{0,8},{8,0},{16,24},{24,16},{1,9},{9,1},{17,25},{25,17},{2,10},{10... | collective-permute-start | bytes 417800 | tf_op jit(solution)/shard_map/ppermute | solution.py:36
  25.7 1.1 %shard_map.108 = (f32[4,256,128]{2,1,0:T(8,128)S(1)}, f32[256,128]{1,0:T(8,128)S(1)}) custom-call(f32[256,128]{1,0:T(8,128)S(1)} %get-tuple-element.40.refs_0_, f32[4,256,128]{2,1,0:T(8,128)S(1)} %get-tuple-element.42.refs_1_, f32[256,128]{1,0:T(8,128)S(1)} %get-tuple-element.43.refs_2_, f32[272,128]{1,0:T(8,128)S(1)} %collective-permute-done.7.refs_3_.refs_10_, ...), custom_call_target="tpu_custom_call" | custom-call | flops 536870912 | bytes 262144 | tf_op jit(solution)/shard_map/pallas_call | solution.py:426
  26.8 0.0 copy-start
  26.8 0.0 copy-start.1
  26.8 0.0 copy-start.2
  26.9 7.4 %shard_map.109 = (f32[72,128]{1,0:T(8,128)S(1)}, f32[72,128]{1,0:T(8,128)S(1)}, f32[72,128]{1,0:T(8,128)S(1)}, f32[72,128]{1,0:T(8,128)S(1)}) custom-call(f32[256,128]{1,0:T(8,128)S(1)} %get-tuple-element.40.refs_0_, f32[4,256,128]{2,1,0:T(8,128)S(1)} %get-tuple-element.46.refs_1_, f32[256,128]{1,0:T(8,128)S(1)} %get-tuple-element.47.refs_2_, ...), custom_call_target="tpu_custom_call" | custom-call | flops 536870912 | bytes 262144 | tf_op jit(solution)/shard_map/pallas_call | solution.py:426
  34.2 1.8 %collective-permute-start.11 = (f32[72,128]{1,0:T(8,128)S(1)}, f32[72,128]{1,0:T(8,128)S(1)}, u32[]{:S(2)}, u32[]{:S(2)}) collective-permute-start(f32[72,128]{1,0:T(8,128)S(1)} %get-tuple-element.50), channel_id=1, source_target_pairs={{0,2},{2,0},{4,6},{6,4},{1,3},{3,1},{5,7},{7,5},{8,10},{10,8},{12,... | collective-permute-start | bytes 110600 | tf_op jit(solution)/shard_map/ppermute | solution.py:36
  36.1 2.6 %collective-permute-start.12 = (f32[72,128]{1,0:T(8,128)S(1)}, f32[72,128]{1,0:T(8,128)S(1)}, u32[]{:S(2)}, u32[]{:S(2)}) collective-permute-start(f32[72,128]{1,0:T(8,128)S(1)} %get-tuple-element.51), channel_id=1, source_target_pairs={{0,4},{2,6},{4,0},{6,2},{1,5},{3,7},{5,1},{7,3},{8,12},{10,14},{12... | collective-permute-start | bytes 110600 | tf_op jit(solution)/shard_map/ppermute | solution.py:36
  38.7 3.0 %collective-permute-done.12.rest_2_ = f32[72,128]{1,0:T(8,128)S(1)} collective-permute-done((f32[72,128]{1,0:T(8,128)S(1)}, f32[72,128]{1,0:T(8,128)S(1)}, u32[]{:S(2)}, u32[]{:S(2)}) %collective-permute-start.12) | collective-permute-done | bytes 36896 | tf_op jit(solution)/shard_map/ppermute | solution.py:36
  41.7 2.7 %collective-permute-done.13.rest_3_ = f32[72,128]{1,0:T(8,128)S(1)} collective-permute-done((f32[72,128]{1,0:T(8,128)S(1)}, f32[72,128]{1,0:T(8,128)S(1)}, u32[]{:S(2)}, u32[]{:S(2)}) %collective-permute-start.13) | collective-permute-done | bytes 36896 | tf_op jit(solution)/shard_map/ppermute | solution.py:36
  44.4 1.1 %shard_map.110 = bf16[64,128]{1,0:T(8,128)(2,1)} custom-call(f32[64,128]{1,0:T(8,128)S(1)} %get-tuple-element.32.zdst_ref, f32[1,128]{1,0:T(1,128)S(1)} %bitcast.7, f32[1,128]{1,0:T(1,128)S(1)} %bitcast.5, f32[1,128]{1,0:T(1,128)S(1)} %bitcast.8, f32[72,128]{1,0:T(8,128)S(1)} %get-tuple-element.49.rest_0_, f32[72,128]{1,0:T(8,128)S(1)} %collective-permute-done.11.rest_1_, ...), custom_call_target="tpu_custom_call" | custom-call | tf_op jit(solution)/shard_map/pallas_call | solution.py:40
  (13 shorter events, 0.0 us)
Async XLA Ops:
  1.2 7.4 %collective-permute-start.5 = (f32[256,128]{1,0:T(8,128)S(1)}, f32[256,128]{1,0:T(8,128)S(1)}, u32[]{:S(2)}, u32[]{:S(2)}) collective-permute-start(f32[256,128]{1,0:T(8,128)S(1)} %get-tuple-element.38), channel_id=1, source_target_pairs={{0,1},{1,0},{2,3},{3,2},{4,5},{5,4},{6,7},{7,6},{8,9},{9,8},{10,11... | collective-permute-start | bytes 393224 | tf_op jit(solution)/shard_map/ppermute | solution.py:36
  4.2 6.3 %collective-permute-start.3 = (f32[256,128]{1,0:T(8,128)S(1)}, f32[256,128]{1,0:T(8,128)S(1)}, u32[]{:S(2)}, u32[]{:S(2)}) collective-permute-start(f32[256,128]{1,0:T(8,128)S(1)} %get-tuple-element.36), channel_id=1, source_target_pairs={{0,1},{1,0},{2,3},{3,2},{4,5},{5,4},{6,7},{7,6},{8,9},{9,8},{10,11... | collective-permute-start | bytes 393224 | tf_op jit(solution)/shard_map/ppermute | solution.py:36
  8.8 14.3 %collective-permute-start.6 = (f32[272,128]{1,0:T(8,128)S(1)}, f32[272,128]{1,0:T(8,128)S(1)}, u32[]{:S(2)}, u32[]{:S(2)}) collective-permute-start(f32[272,128]{1,0:T(8,128)S(1)} %shard_map.105.refs_4_.refs_8_), channel_id=1, source_target_pairs={{0,8},{8,0},{16,24},{24,16},{1,9},{9,1},{17,25},{25,17},{2,10},{10... | collective-permute-start | bytes 417800 | tf_op jit(solution)/shard_map/ppermute | solution.py:36
  10.7 12.3 %collective-permute-start.4 = (f32[272,128]{1,0:T(8,128)S(1)}, f32[272,128]{1,0:T(8,128)S(1)}, u32[]{:S(2)}, u32[]{:S(2)}) collective-permute-start(f32[272,128]{1,0:T(8,128)S(1)} %shard_map.104.refs_2_.refs_6_), channel_id=1, source_target_pairs={{0,8},{8,0},{16,24},{24,16},{1,9},{9,1},{17,25},{25,17},{2,10},{10... | collective-permute-start | bytes 417800 | tf_op jit(solution)/shard_map/ppermute | solution.py:36
  10.7 4.0 %collective-permute-start = (f32[64,128]{1,0:T(8,128)S(1)}, f32[64,128]{1,0:T(8,128)S(1)}, u32[]{:S(2)}, u32[]{:S(2)}) collective-permute-start(f32[64,128]{1,0:T(8,128)S(1)} %get-tuple-element.31), channel_id=1, source_target_pairs={{0,1},{1,0},{2,3},{3,2},{4,5},{5,4},{6,7},{7,6},{8,9},{9,8},{10,11... | collective-permute-start | bytes 98312 | tf_op jit(solution)/shard_map/ppermute | solution.py:36
  12.5 12.6 %collective-permute-start.8 = (f32[272,128]{1,0:T(8,128)S(1)}, f32[272,128]{1,0:T(8,128)S(1)}, u32[]{:S(2)}, u32[]{:S(2)}) collective-permute-start(f32[272,128]{1,0:T(8,128)S(1)} %shard_map.105.refs_4_.refs_8_), channel_id=1, source_target_pairs={{0,16},{8,24},{16,0},{24,8},{1,17},{9,25},{17,1},{25,9},{2,18},{10... | collective-permute-start | bytes 417800 | tf_op jit(solution)/shard_map/ppermute | solution.py:36
  14.0 11.1 %collective-permute-start.7 = (f32[272,128]{1,0:T(8,128)S(1)}, f32[272,128]{1,0:T(8,128)S(1)}, u32[]{:S(2)}, u32[]{:S(2)}) collective-permute-start(f32[272,128]{1,0:T(8,128)S(1)} %shard_map.104.refs_2_.refs_6_), channel_id=1, source_target_pairs={{0,16},{8,24},{16,0},{24,8},{1,17},{9,25},{17,1},{25,9},{2,18},{10... | collective-permute-start | bytes 417800 | tf_op jit(solution)/shard_map/ppermute | solution.py:36
  14.8 4.5 %collective-permute-start.1 = (f32[8,64]{1,0:T(8,128)S(1)}, f32[8,64]{1,0:T(8,128)S(1)}, u32[]{:S(2)}, u32[]{:S(2)}) collective-permute-start(f32[8,64]{1,0:T(8,128)S(1)} %get-tuple-element.33.low_ref), channel_id=1, source_target_pairs={{0,4},{2,6},{4,0},{6,2},{1,5},{3,7},{5,1},{7,3},{8,12},{10,14},{12... | collective-permute-start | bytes 6152 | tf_op jit(solution)/shard_map/ppermute | solution.py:36
  19.4 3.7 %collective-permute-start.2 = (f32[16,64]{1,0:T(8,128)S(1)}, f32[16,64]{1,0:T(8,128)S(1)}, u32[]{:S(2)}, u32[]{:S(2)}) collective-permute-start(f32[16,64]{1,0:T(8,128)S(1)} %shard_map.102.refs_0_), channel_id=1, source_target_pairs={{0,2},{2,0},{4,6},{6,4},{1,3},{3,1},{5,7},{7,5},{8,10},{10,8},{12,... | collective-permute-start | bytes 12296 | tf_op jit(solution)/shard_map/ppermute | solution.py:36
  25.1 1.7 %collective-permute-start.9 = (f32[272,128]{1,0:T(8,128)S(1)}, f32[272,128]{1,0:T(8,128)S(1)}, u32[]{:S(2)}, u32[]{:S(2)}) collective-permute-start(f32[272,128]{1,0:T(8,128)S(1)} %collective-permute-done.7.refs_3_.refs_10_), channel_id=1, source_target_pairs={{0,8},{8,0},{16,24},{24,16},{1,9},{9,1},{17,25},{25,17},{2,10},{10... | collective-permute-start | bytes 417800 | tf_op jit(solution)/shard_map/ppermute | solution.py:36
  25.2 1.6 %collective-permute-start.10 = (f32[272,128]{1,0:T(8,128)S(1)}, f32[272,128]{1,0:T(8,128)S(1)}, u32[]{:S(2)}, u32[]{:S(2)}) collective-permute-start(f32[272,128]{1,0:T(8,128)S(1)} %collective-permute-done.8.refs_4_.refs_11_), channel_id=1, source_target_pairs={{0,8},{8,0},{16,24},{24,16},{1,9},{9,1},{17,25},{25,17},{2,10},{10... | collective-permute-start | bytes 417800 | tf_op jit(solution)/shard_map/ppermute | solution.py:36
  26.8 17.6 %copy-start = (f32[128]{0:T(128)S(1)}, f32[128]{0:T(128)}, u32[]{:S(2)}) copy-start(f32[128]{0:T(128)} %param.14) | copy-start | bytes 1540
  26.8 17.6 %copy-start.1 = (f32[128]{0:T(128)S(1)}, f32[128]{0:T(128)}, u32[]{:S(2)}) copy-start(f32[128]{0:T(128)} %param.13) | copy-start | bytes 1540
  26.8 17.6 %copy-start.2 = (f32[128]{0:T(128)S(1)}, f32[128]{0:T(128)}, u32[]{:S(2)}) copy-start(f32[128]{0:T(128)} %param.15) | copy-start | bytes 1540
  34.2 4.4 %collective-permute-start.11 = (f32[72,128]{1,0:T(8,128)S(1)}, f32[72,128]{1,0:T(8,128)S(1)}, u32[]{:S(2)}, u32[]{:S(2)}) collective-permute-start(f32[72,128]{1,0:T(8,128)S(1)} %get-tuple-element.50), channel_id=1, source_target_pairs={{0,2},{2,0},{4,6},{6,4},{1,3},{3,1},{5,7},{7,5},{8,10},{10,8},{12,... | collective-permute-start | bytes 110600 | tf_op jit(solution)/shard_map/ppermute | solution.py:36
  36.1 5.6 %collective-permute-start.12 = (f32[72,128]{1,0:T(8,128)S(1)}, f32[72,128]{1,0:T(8,128)S(1)}, u32[]{:S(2)}, u32[]{:S(2)}) collective-permute-start(f32[72,128]{1,0:T(8,128)S(1)} %get-tuple-element.51), channel_id=1, source_target_pairs={{0,4},{2,6},{4,0},{6,2},{1,5},{3,7},{5,1},{7,3},{8,12},{10,14},{12... | collective-permute-start | bytes 110600 | tf_op jit(solution)/shard_map/ppermute | solution.py:36
  38.7 5.8 %collective-permute-start.13 = (f32[72,128]{1,0:T(8,128)S(1)}, f32[72,128]{1,0:T(8,128)S(1)}, u32[]{:S(2)}, u32[]{:S(2)}) collective-permute-start(f32[72,128]{1,0:T(8,128)S(1)} %get-tuple-element.52), channel_id=1, source_target_pairs={{0,6},{2,4},{4,2},{6,0},{1,7},{3,5},{5,3},{7,1},{8,14},{10,12},{12... | collective-permute-start | bytes 110600 | tf_op jit(solution)/shard_map/ppermute | solution.py:36
where the time goes:
time: 45.7 us; the launch traced here: 45.5 us
  Pallas kernels  17.1 us (37%)
  starting transfers between devices  16.6 us (36%)
  waiting for transfers between devices  11 us (24%)
  between operations  0.79 us (2%)
    ppermute x14, starting transfers between devices, hop(): return lax.ppermute(x, axis, pairs)  16.6 us
    ppermute x14, waiting for transfers between devices, hop(): return lax.ppermute(x, axis, pairs)  11 us
    pallas_call x3, Pallas kernels, stage(): pl.pallas_call(kernel, out_shape=[pltpu.VMEM(s, F32) for s in outs], grid...  10.6 us
    pallas_call x8, Pallas kernels, call(): pl.pallas_call(kernel, out_shape=out_shape, in_specs=in_specs or [VMEM] *...  6.6 us
  transfers between devices with their start and end apart: 14, of which 6 were waited for; matrix products, arithmetic and copies ran while one was open for 0% of the time, Pallas kernels for 16%

commit v1 on v0

--- a/solution.py
+++ b/solution.py
@@ -166,7 +166,7 @@
     tiles = row_tiles * col_tiles
     whole = lambda shape: pl.BlockSpec(shape, lambda s: (0,) * len(shape))
 
-    def dst_kernel(own_ref, att_ref, *rest):
+    def dst_kernel(own_ref, att_ref, _, *rest):
         got, (z_ref, s_ref) = rest[: n_feat - 1], rest[n_feat - 1 :]
         z = own_ref[...]
         for part in got:
@@ -182,7 +182,9 @@
         ],
         dst_own,
         dst_att,
+        tile_count,
         *dst_parts,
+        in_specs=[VMEM, VMEM, SMEM] + [VMEM] * len(dst_parts),
     )
     rows_of = up8(heads)
     if is_pow2(n_col) and n_col > 1:
@@ -606,12 +608,12 @@
         z = zdst_ref[...]
         pair = contract(z * (dst_ref[...] + src_ref[...]), same, ((1,), (0,)))
         e_self = leaky(LOG2E * pair)
-        which = lax.broadcasted_iota(jnp.int32, (mdp, width), 0)
-        head = lax.broadcasted_iota(jnp.int32, (mdp, width), 1) // dims
-        den_of, m_of = (which == head).astype(F32), (which == head + heads).astype(F32)
+        which = lax.broadcasted_iota(jnp.int32, (mdp, 2 * width), 0)
+        lane = lax.broadcasted_iota(jnp.int32, (mdp, 2 * width), 1)
+        pick = (which == jnp.where(lane < width, heads + lane // dims, (lane - width) // dims)).astype(F32)
         mds = [part[own_rows:, :own_rows] for part in parts]
-        ms = [contract(md, m_of, ((0,), (0,))) for md in mds]
-        dens = [contract(md, den_of, ((0,), (0,))) for md in mds]
+        both = [contract(md, pick, ((0,), (0,))) for md in mds]
+        ms, dens = [b[:, :width] for b in both], [b[:, width:] for b in both]
         top = e_self
         for m in ms:
             top = jnp.maximum(top, m)

time: 45.7 us -> 45.7 us (level)
  no operation moved by 1% of the time
where the time goes in v1:
time: 45.7 us; the launch traced here: 45.6 us
  Pallas kernels  17.2 us (38%)
  starting transfers between devices  16.6 us (36%)
  waiting for transfers between devices  11 us (24%)
  between operations  0.79 us (2%)
    ppermute x14, starting transfers between devices, hop(): return lax.ppermute(x, axis, pairs)  16.6 us
    ppermute x14, waiting for transfers between devices, hop(): return lax.ppermute(x, axis, pairs)  11 us
    pallas_call x3, Pallas kernels, stage(): pl.pallas_call(kernel, out_shape=[pltpu.VMEM(s, F32) for s in outs], grid...  10.6 us
    pallas_call x8, Pallas kernels, call(): pl.pallas_call(kernel, out_shape=out_shape, in_specs=in_specs or [VMEM] *...  6.63 us
  transfers between devices with their start and end apart: 14, of which 6 were waited for; matrix products, arithmetic and copies ran while one was open for 0% of the time, Pallas kernels for 16%

profile of v1, /device:TPU:0, one launch (start us, length us, event | category | flops | bytes accessed | tf_op | source)
XLA Modules:
  0.0 45.6 jit_solution(2908826803810499626)
XLA Ops:
  0.0 1.2 %shard_map.100 = (f32[64,128]{1,0:T(8,128)S(1)}, f32[8,128]{1,0:T(8,128)S(1)}, f32[64,128]{1,0:T(8,128)S(1)}, f32[256,128]{1,0:T(8,128)S(1)}, f32[256,128]{1,0:T(8,128)S(1)}) custom-call(bf16[512,128]{1,0:T(8,128)(2,1)} %refs_0_.4, bf16[64,128]{1,0:T(8,128)(2,1)} %refs_1_.3, bf16[128,256]{1,0:T(8,128)(2,1)} %refs_1_.4, f32[1,128]{1,0:T(1,128)} %bitcast.4), custom_call_target="tpu_custom_call" | custom-call | tf_op jit(solution)/shard_map/pallas_call | solution.py:40
  1.2 3.0 %collective-permute-start.5 = (f32[256,128]{1,0:T(8,128)S(1)}, f32[256,128]{1,0:T(8,128)S(1)}, u32[]{:S(2)}, u32[]{:S(2)}) collective-permute-start(f32[256,128]{1,0:T(8,128)S(1)} %get-tuple-element.38), channel_id=1, source_target_pairs={{0,1},{1,0},{2,3},{3,2},{4,5},{5,4},{6,7},{7,6},{8,9},{9,8},{10,11... | collective-permute-start | bytes 393224 | tf_op jit(solution)/shard_map/ppermute | solution.py:36
  4.2 0.1 collective-permute-start.3
  4.9 2.0 %shard_map.103 = (f32[8,128]{1,0:T(8,128)S(1)}, f32[256,128]{1,0:T(8,128)S(1)}, f32[256,128]{1,0:T(8,128)S(1)}, f32[8,2,2,128,128]{4,3,2,1,0:T(8,128)S(1)}) custom-call(bf16[512,128]{1,0:T(8,128)(2,1)} %refs_0_.4, bf16[128,256]{1,0:T(8,128)(2,1)} %refs_1_.4, f32[1,128]{1,0:T(1,128)} %bitcast.6, s32[1,1,128]{2,1,0:T(1,128)} %refs_0_.5, s32[1,1,128]{2,1,0:T(1,128)} %refs_1_.5, ...), custom_call_target="tpu_custom_call" | custom-call | tf_op jit(solution)/shard_map/pallas_call | solution.py:40
  6.9 1.6 %collective-permute-done.5.rest_0_ = f32[256,128]{1,0:T(8,128)S(1)} collective-permute-done((f32[256,128]{1,0:T(8,128)S(1)}, f32[256,128]{1,0:T(8,128)S(1)}, u32[]{:S(2)}, u32[]{:S(2)}) %collective-permute-start.5) | collective-permute-done | bytes 131104 | tf_op jit(solution)/shard_map/ppermute | solution.py:36
  8.6 0.2 shard_map.105.refs_4_.refs_8_
  8.8 0.0 collective-permute-start.6
  8.8 1.8 %collective-permute-done.3.rest_0_ = f32[256,128]{1,0:T(8,128)S(1)} collective-permute-done((f32[256,128]{1,0:T(8,128)S(1)}, f32[256,128]{1,0:T(8,128)S(1)}, u32[]{:S(2)}, u32[]{:S(2)}) %collective-permute-start.3) | collective-permute-done | bytes 131104 | tf_op jit(solution)/shard_map/ppermute | solution.py:36
  10.5 0.2 shard_map.104.refs_2_.refs_6_
  10.7 1.8 %collective-permute-start = (f32[64,128]{1,0:T(8,128)S(1)}, f32[64,128]{1,0:T(8,128)S(1)}, u32[]{:S(2)}, u32[]{:S(2)}) collective-permute-start(f32[64,128]{1,0:T(8,128)S(1)} %get-tuple-element.31), channel_id=1, source_target_pairs={{0,1},{1,0},{2,3},{3,2},{4,5},{5,4},{6,7},{7,6},{8,9},{9,8},{10,11... | collective-permute-start | bytes 98312 | tf_op jit(solution)/shard_map/ppermute | solution.py:36
  12.5 1.5 %collective-permute-start.8 = (f32[272,128]{1,0:T(8,128)S(1)}, f32[272,128]{1,0:T(8,128)S(1)}, u32[]{:S(2)}, u32[]{:S(2)}) collective-permute-start(f32[272,128]{1,0:T(8,128)S(1)} %shard_map.105.refs_4_.refs_8_), channel_id=1, source_target_pairs={{0,16},{8,24},{16,0},{24,8},{1,17},{9,25},{17,1},{25,9},{2,18},{10... | collective-permute-start | bytes 417800 | tf_op jit(solution)/shard_map/ppermute | solution.py:36
  14.0 0.5 %collective-permute-start.7 = (f32[272,128]{1,0:T(8,128)S(1)}, f32[272,128]{1,0:T(8,128)S(1)}, u32[]{:S(2)}, u32[]{:S(2)}) collective-permute-start(f32[272,128]{1,0:T(8,128)S(1)} %shard_map.104.refs_2_.refs_6_), channel_id=1, source_target_pairs={{0,16},{8,24},{16,0},{24,8},{1,17},{9,25},{17,1},{25,9},{2,18},{10... | collective-permute-start | bytes 417800 | tf_op jit(solution)/shard_map/ppermute | solution.py:36
  14.5 0.1 collective-permute-done.rest_0_
  14.7 0.1 shard_map.101
  14.8 2.9 %collective-permute-start.1 = (f32[8,64]{1,0:T(8,128)S(1)}, f32[8,64]{1,0:T(8,128)S(1)}, u32[]{:S(2)}, u32[]{:S(2)}) collective-permute-start(f32[8,64]{1,0:T(8,128)S(1)} %get-tuple-element.33.low_ref), channel_id=1, source_target_pairs={{0,4},{2,6},{4,0},{6,2},{1,5},{3,7},{5,1},{7,3},{8,12},{10,14},{12... | collective-permute-start | bytes 6152 | tf_op jit(solution)/shard_map/ppermute | solution.py:36
  17.7 1.7 %collective-permute-done.1.high_ref = f32[8,64]{1,0:T(8,128)S(1)} collective-permute-done((f32[8,64]{1,0:T(8,128)S(1)}, f32[8,64]{1,0:T(8,128)S(1)}, u32[]{:S(2)}, u32[]{:S(2)}) %collective-permute-start.1) | collective-permute-done | bytes 2080 | tf_op jit(solution)/shard_map/ppermute | solution.py:36
  19.4 1.8 %collective-permute-start.2 = (f32[16,64]{1,0:T(8,128)S(1)}, f32[16,64]{1,0:T(8,128)S(1)}, u32[]{:S(2)}, u32[]{:S(2)}) collective-permute-start(f32[16,64]{1,0:T(8,128)S(1)} %shard_map.102.refs_0_), channel_id=1, source_target_pairs={{0,2},{2,0},{4,6},{6,4},{1,3},{3,1},{5,7},{7,5},{8,10},{10,8},{12,... | collective-permute-start | bytes 12296 | tf_op jit(solution)/shard_map/ppermute | solution.py:36
  21.2 1.8 %shard_map.106.refs_7_.refs_9_.refs_11_.refs_13_.refs_6_.refs_8_.refs_15_.refs_17_.refs_19_.refs_21_.refs_23_.refs_25_.refs_27_ = f32[8,2,2,128,128]{4,3,2,1,0:T(8,128)S(1)} custom-call(s32[1,1,128]{2,1,0:T(1,128)} %refs_0_.5, s32[1,1,128]{2,1,0:T(1,128)} %refs_1_.5, bf16[4,32,128,128]{3,2,1,0:T(8,128)(2,1)} %bitcast.10, s32[1,1]{1,0:T(1,128)S(6)} %copy.11._.refs_6_.refs_3_), custom_call_target="tpu_custom_call" | custom-call | tf_op jit(solution)/shard_map/pallas_call | solution.py:40
  23.0 0.0 collective-permute-done.2.refs_1_
  23.0 2.1 %shard_map.107 = (f32[256,128]{1,0:T(8,128)S(1)}, f32[256,128]{1,0:T(8,128)S(1)}, f32[4,256,128]{2,1,0:T(8,128)S(1)}, f32[256,128]{1,0:T(8,128)S(1)}) custom-call(f32[16,64]{1,0:T(8,128)S(1)} %shard_map.102.refs_0_, f32[16,64]{1,0:T(8,128)S(1)} %collective-permute-done.2.refs_1_, f32[272,128]{1,0:T(8,128)S(1)} %shard_map.104.refs_2_.refs_6_, ...), custom_call_target="tpu_custom_call" | custom-call | flops 1073741824 | bytes 524288 | tf_op jit(solution)/shard_map/pallas_call | solution.py:428
  25.1 0.1 collective-permute-start.9
  25.2 0.5 %collective-permute-start.10 = (f32[272,128]{1,0:T(8,128)S(1)}, f32[272,128]{1,0:T(8,128)S(1)}, u32[]{:S(2)}, u32[]{:S(2)}) collective-permute-start(f32[272,128]{1,0:T(8,128)S(1)} %collective-permute-done.8.refs_4_.refs_11_), channel_id=1, source_target_pairs={{0,8},{8,0},{16,24},{24,16},{1,9},{9,1},{17,25},{25,17},{2,10},{10... | collective-permute-start | bytes 417800 | tf_op jit(solution)/shard_map/ppermute | solution.py:36
  25.7 1.1 %shard_map.108 = (f32[4,256,128]{2,1,0:T(8,128)S(1)}, f32[256,128]{1,0:T(8,128)S(1)}) custom-call(f32[256,128]{1,0:T(8,128)S(1)} %get-tuple-element.40.refs_0_, f32[4,256,128]{2,1,0:T(8,128)S(1)} %get-tuple-element.42.refs_1_, f32[256,128]{1,0:T(8,128)S(1)} %get-tuple-element.43.refs_2_, f32[272,128]{1,0:T(8,128)S(1)} %collective-permute-done.7.refs_3_.refs_10_, ...), custom_call_target="tpu_custom_call" | custom-call | flops 536870912 | bytes 262144 | tf_op jit(solution)/shard_map/pallas_call | solution.py:428
  26.8 0.0 copy-start
  26.8 0.0 copy-start.1
  26.8 0.0 copy-start.2
  26.9 7.4 %shard_map.109 = (f32[72,128]{1,0:T(8,128)S(1)}, f32[72,128]{1,0:T(8,128)S(1)}, f32[72,128]{1,0:T(8,128)S(1)}, f32[72,128]{1,0:T(8,128)S(1)}) custom-call(f32[256,128]{1,0:T(8,128)S(1)} %get-tuple-element.40.refs_0_, f32[4,256,128]{2,1,0:T(8,128)S(1)} %get-tuple-element.46.refs_1_, f32[256,128]{1,0:T(8,128)S(1)} %get-tuple-element.47.refs_2_, ...), custom_call_target="tpu_custom_call" | custom-call | flops 536870912 | bytes 262144 | tf_op jit(solution)/shard_map/pallas_call | solution.py:428
  34.2 1.8 %collective-permute-start.11 = (f32[72,128]{1,0:T(8,128)S(1)}, f32[72,128]{1,0:T(8,128)S(1)}, u32[]{:S(2)}, u32[]{:S(2)}) collective-permute-start(f32[72,128]{1,0:T(8,128)S(1)} %get-tuple-element.50), channel_id=1, source_target_pairs={{0,2},{2,0},{4,6},{6,4},{1,3},{3,1},{5,7},{7,5},{8,10},{10,8},{12,... | collective-permute-start | bytes 110600 | tf_op jit(solution)/shard_map/ppermute | solution.py:36
  36.1 2.6 %collective-permute-start.12 = (f32[72,128]{1,0:T(8,128)S(1)}, f32[72,128]{1,0:T(8,128)S(1)}, u32[]{:S(2)}, u32[]{:S(2)}) collective-permute-start(f32[72,128]{1,0:T(8,128)S(1)} %get-tuple-element.51), channel_id=1, source_target_pairs={{0,4},{2,6},{4,0},{6,2},{1,5},{3,7},{5,1},{7,3},{8,12},{10,14},{12... | collective-permute-start | bytes 110600 | tf_op jit(solution)/shard_map/ppermute | solution.py:36
  38.7 3.0 %collective-permute-done.12.rest_2_ = f32[72,128]{1,0:T(8,128)S(1)} collective-permute-done((f32[72,128]{1,0:T(8,128)S(1)}, f32[72,128]{1,0:T(8,128)S(1)}, u32[]{:S(2)}, u32[]{:S(2)}) %collective-permute-start.12) | collective-permute-done | bytes 36896 | tf_op jit(solution)/shard_map/ppermute | solution.py:36
  41.7 2.7 %collective-permute-done.13.rest_3_ = f32[72,128]{1,0:T(8,128)S(1)} collective-permute-done((f32[72,128]{1,0:T(8,128)S(1)}, f32[72,128]{1,0:T(8,128)S(1)}, u32[]{:S(2)}, u32[]{:S(2)}) %collective-permute-start.13) | collective-permute-done | bytes 36896 | tf_op jit(solution)/shard_map/ppermute | solution.py:36
  44.4 1.1 %shard_map.110 = bf16[64,128]{1,0:T(8,128)(2,1)} custom-call(f32[64,128]{1,0:T(8,128)S(1)} %get-tuple-element.32.zdst_ref, f32[1,128]{1,0:T(1,128)S(1)} %bitcast.7, f32[1,128]{1,0:T(1,128)S(1)} %bitcast.5, f32[1,128]{1,0:T(1,128)S(1)} %bitcast.8, f32[72,128]{1,0:T(8,128)S(1)} %get-tuple-element.49.rest_0_, f32[72,128]{1,0:T(8,128)S(1)} %collective-permute-done.11.rest_1_, ...), custom_call_target="tpu_custom_call" | custom-call | tf_op jit(solution)/shard_map/pallas_call | solution.py:40
  (13 shorter events, 0.0 us)
Async XLA Ops:
  1.2 7.4 %collective-permute-start.5 = (f32[256,128]{1,0:T(8,128)S(1)}, f32[256,128]{1,0:T(8,128)S(1)}, u32[]{:S(2)}, u32[]{:S(2)}) collective-permute-start(f32[256,128]{1,0:T(8,128)S(1)} %get-tuple-element.38), channel_id=1, source_target_pairs={{0,1},{1,0},{2,3},{3,2},{4,5},{5,4},{6,7},{7,6},{8,9},{9,8},{10,11... | collective-permute-start | bytes 393224 | tf_op jit(solution)/shard_map/ppermute | solution.py:36
  4.2 6.3 %collective-permute-start.3 = (f32[256,128]{1,0:T(8,128)S(1)}, f32[256,128]{1,0:T(8,128)S(1)}, u32[]{:S(2)}, u32[]{:S(2)}) collective-permute-start(f32[256,128]{1,0:T(8,128)S(1)} %get-tuple-element.36), channel_id=1, source_target_pairs={{0,1},{1,0},{2,3},{3,2},{4,5},{5,4},{6,7},{7,6},{8,9},{9,8},{10,11... | collective-permute-start | bytes 393224 | tf_op jit(solution)/shard_map/ppermute | solution.py:36
  8.8 14.3 %collective-permute-start.6 = (f32[272,128]{1,0:T(8,128)S(1)}, f32[272,128]{1,0:T(8,128)S(1)}, u32[]{:S(2)}, u32[]{:S(2)}) collective-permute-start(f32[272,128]{1,0:T(8,128)S(1)} %shard_map.105.refs_4_.refs_8_), channel_id=1, source_target_pairs={{0,8},{8,0},{16,24},{24,16},{1,9},{9,1},{17,25},{25,17},{2,10},{10... | collective-permute-start | bytes 417800 | tf_op jit(solution)/shard_map/ppermute | solution.py:36
  10.7 12.3 %collective-permute-start.4 = (f32[272,128]{1,0:T(8,128)S(1)}, f32[272,128]{1,0:T(8,128)S(1)}, u32[]{:S(2)}, u32[]{:S(2)}) collective-permute-start(f32[272,128]{1,0:T(8,128)S(1)} %shard_map.104.refs_2_.refs_6_), channel_id=1, source_target_pairs={{0,8},{8,0},{16,24},{24,16},{1,9},{9,1},{17,25},{25,17},{2,10},{10... | collective-permute-start | bytes 417800 | tf_op jit(solution)/shard_map/ppermute | solution.py:36
  10.7 4.0 %collective-permute-start = (f32[64,128]{1,0:T(8,128)S(1)}, f32[64,128]{1,0:T(8,128)S(1)}, u32[]{:S(2)}, u32[]{:S(2)}) collective-permute-start(f32[64,128]{1,0:T(8,128)S(1)} %get-tuple-element.31), channel_id=1, source_target_pairs={{0,1},{1,0},{2,3},{3,2},{4,5},{5,4},{6,7},{7,6},{8,9},{9,8},{10,11... | collective-permute-start | bytes 98312 | tf_op jit(solution)/shard_map/ppermute | solution.py:36
  12.5 12.6 %collective-permute-start.8 = (f32[272,128]{1,0:T(8,128)S(1)}, f32[272,128]{1,0:T(8,128)S(1)}, u32[]{:S(2)}, u32[]{:S(2)}) collective-permute-start(f32[272,128]{1,0:T(8,128)S(1)} %shard_map.105.refs_4_.refs_8_), channel_id=1, source_target_pairs={{0,16},{8,24},{16,0},{24,8},{1,17},{9,25},{17,1},{25,9},{2,18},{10... | collective-permute-start | bytes 417800 | tf_op jit(solution)/shard_map/ppermute | solution.py:36
  14.0 11.1 %collective-permute-start.7 = (f32[272,128]{1,0:T(8,128)S(1)}, f32[272,128]{1,0:T(8,128)S(1)}, u32[]{:S(2)}, u32[]{:S(2)}) collective-permute-start(f32[272,128]{1,0:T(8,128)S(1)} %shard_map.104.refs_2_.refs_6_), channel_id=1, source_target_pairs={{0,16},{8,24},{16,0},{24,8},{1,17},{9,25},{17,1},{25,9},{2,18},{10... | collective-permute-start | bytes 417800 | tf_op jit(solution)/shard_map/ppermute | solution.py:36
  14.8 4.5 %collective-permute-start.1 = (f32[8,64]{1,0:T(8,128)S(1)}, f32[8,64]{1,0:T(8,128)S(1)}, u32[]{:S(2)}, u32[]{:S(2)}) collective-permute-start(f32[8,64]{1,0:T(8,128)S(1)} %get-tuple-element.33.low_ref), channel_id=1, source_target_pairs={{0,4},{2,6},{4,0},{6,2},{1,5},{3,7},{5,1},{7,3},{8,12},{10,14},{12... | collective-permute-start | bytes 6152 | tf_op jit(solution)/shard_map/ppermute | solution.py:36
  19.4 3.7 %collective-permute-start.2 = (f32[16,64]{1,0:T(8,128)S(1)}, f32[16,64]{1,0:T(8,128)S(1)}, u32[]{:S(2)}, u32[]{:S(2)}) collective-permute-start(f32[16,64]{1,0:T(8,128)S(1)} %shard_map.102.refs_0_), channel_id=1, source_target_pairs={{0,2},{2,0},{4,6},{6,4},{1,3},{3,1},{5,7},{7,5},{8,10},{10,8},{12,... | collective-permute-start | bytes 12296 | tf_op jit(solution)/shard_map/ppermute | solution.py:36
  25.1 1.7 %collective-permute-start.9 = (f32[272,128]{1,0:T(8,128)S(1)}, f32[272,128]{1,0:T(8,128)S(1)}, u32[]{:S(2)}, u32[]{:S(2)}) collective-permute-start(f32[272,128]{1,0:T(8,128)S(1)} %collective-permute-done.7.refs_3_.refs_10_), channel_id=1, source_target_pairs={{0,8},{8,0},{16,24},{24,16},{1,9},{9,1},{17,25},{25,17},{2,10},{10... | collective-permute-start | bytes 417800 | tf_op jit(solution)/shard_map/ppermute | solution.py:36
  25.2 1.6 %collective-permute-start.10 = (f32[272,128]{1,0:T(8,128)S(1)}, f32[272,128]{1,0:T(8,128)S(1)}, u32[]{:S(2)}, u32[]{:S(2)}) collective-permute-start(f32[272,128]{1,0:T(8,128)S(1)} %collective-permute-done.8.refs_4_.refs_11_), channel_id=1, source_target_pairs={{0,8},{8,0},{16,24},{24,16},{1,9},{9,1},{17,25},{25,17},{2,10},{10... | collective-permute-start | bytes 417800 | tf_op jit(solution)/shard_map/ppermute | solution.py:36
  26.8 17.6 %copy-start = (f32[128]{0:T(128)S(1)}, f32[128]{0:T(128)}, u32[]{:S(2)}) copy-start(f32[128]{0:T(128)} %param.14) | copy-start | bytes 1540
  26.8 17.6 %copy-start.1 = (f32[128]{0:T(128)S(1)}, f32[128]{0:T(128)}, u32[]{:S(2)}) copy-start(f32[128]{0:T(128)} %param.13) | copy-start | bytes 1540
  26.8 17.6 %copy-start.2 = (f32[128]{0:T(128)S(1)}, f32[128]{0:T(128)}, u32[]{:S(2)}) copy-start(f32[128]{0:T(128)} %param.15) | copy-start | bytes 1540
  34.2 4.4 %collective-permute-start.11 = (f32[72,128]{1,0:T(8,128)S(1)}, f32[72,128]{1,0:T(8,128)S(1)}, u32[]{:S(2)}, u32[]{:S(2)}) collective-permute-start(f32[72,128]{1,0:T(8,128)S(1)} %get-tuple-element.50), channel_id=1, source_target_pairs={{0,2},{2,0},{4,6},{6,4},{1,3},{3,1},{5,7},{7,5},{8,10},{10,8},{12,... | collective-permute-start | bytes 110600 | tf_op jit(solution)/shard_map/ppermute | solution.py:36
  36.1 5.6 %collective-permute-start.12 = (f32[72,128]{1,0:T(8,128)S(1)}, f32[72,128]{1,0:T(8,128)S(1)}, u32[]{:S(2)}, u32[]{:S(2)}) collective-permute-start(f32[72,128]{1,0:T(8,128)S(1)} %get-tuple-element.51), channel_id=1, source_target_pairs={{0,4},{2,6},{4,0},{6,2},{1,5},{3,7},{5,1},{7,3},{8,12},{10,14},{12... | collective-permute-start | bytes 110600 | tf_op jit(solution)/shard_map/ppermute | solution.py:36
  38.7 5.8 %collective-permute-start.13 = (f32[72,128]{1,0:T(8,128)S(1)}, f32[72,128]{1,0:T(8,128)S(1)}, u32[]{:S(2)}, u32[]{:S(2)}) collective-permute-start(f32[72,128]{1,0:T(8,128)S(1)} %get-tuple-element.52), channel_id=1, source_target_pairs={{0,6},{2,4},{4,2},{6,0},{1,7},{3,5},{5,3},{7,1},{8,14},{10,12},{12... | collective-permute-start | bytes 110600 | tf_op jit(solution)/shard_map/ppermute | solution.py:36
